TPU v7x, 32 devices: a whole 2x2x4 slice. The times are simulated.
32 devices in a mesh: tenant: 4 (over x, core), fsdp: 8 (over z, y).
Axes of the slice: x: 2, y: 2, z: 4, core: 2. Of those that a mesh axis runs over, the one named last changes fastest.
Arguments:
- tokens: bfloat16 [16384, 8192], P(('tenant', 'fsdp')), may hold values from -6 to 6
- cotangent: bfloat16 [16384, 1024], P(('tenant', 'fsdp')), may hold values from -6 to 6
- value_weight: bfloat16 [8192, 1024], P('fsdp'), may hold values from -0.0625 to 0.0625
- adapters: float32 [64, 16, 9216], P('tenant', None, 'fsdp'), may hold values from -2.5 to 2.5
- first_moment: float32 [64, 16, 9216], P('tenant', None, 'fsdp'), may hold values from -4 to 4
- second_moment: float32 [64, 16, 9216], P('tenant', None, 'fsdp'), may hold values from 0.2 to 2
- tenant_home: int32 [64], replicated, may hold values from 0 to 63, as said below
- read_tenants: int32 [32, 4], replicated, may hold values from 0 to 63, as said below
- row_tenant: int32 [16384], P(('tenant', 'fsdp')), may hold values from 0 to 63, as said below
Outputs:
- values: bfloat16 [16384, 1024], P(('tenant', 'fsdp'))
- token_grad: bfloat16 [16384, 8192], P(('tenant', 'fsdp'))
- new_adapters: float32 [64, 16, 9216], P('tenant', None, 'fsdp')
- new_first: float32 [64, 16, 9216], P('tenant', None, 'fsdp')
- new_second: float32 [64, 16, 9216], P('tenant', None, 'fsdp')
- refreshed: bfloat16 [128, 16, 9216], P(('tenant', 'fsdp'))
Inputs may be any that keep to these rules, and one draw needn't show every extreme that they name: `tenant_home`: a permutation: every slot holds exactly one tenant; slot h belongs to index h // 16 of tenant. `read_tenants`: in each row, entry k is a tenant whose slot lies in index k of tenant. `row_tenant`: every row's tenant is in the read list of its block, and every entry of a block's read list is the tenant of some row of that block.
All inputs are finite; a program needn't handle non-finite values.
Results may differ from a plain program's by a relative error of at most 0.0055.
Values may be sent and summed in bfloat16 or wider, within the bound.
A program may use at most 128 MiB of HBM per device.

v0:
```python
import math

import jax
import jax.numpy as jnp
from jax import lax
from jax.sharding import PartitionSpec as P

beta_first = 0.9
beta_second = 0.95
learn_rate = 0.1
adam_eps = 1e-08
corr_first = 1.0 - 0.9**10
corr_second = 1.0 - 0.95**10


def bring_back(selected_rows, tenant_total, shard_count, tenants_per_owner):
    adapter_rank_size = selected_rows.shape[1]
    section_width = selected_rows.shape[2]
    received_rows = lax.all_to_all(
        selected_rows, ("tenant", "fsdp"), split_axis=0, concat_axis=0, tiled=True
    )
    received_rows = received_rows.reshape(
        tenant_total, shard_count, tenants_per_owner, adapter_rank_size, section_width
    )
    received_rows = received_rows.transpose(0, 2, 3, 1, 4)
    return received_rows.reshape(
        tenant_total * tenants_per_owner, adapter_rank_size, shard_count * section_width
    )


def per_device(
    tokens,
    cotangent,
    value_weight,
    adapters,
    first_moment,
    second_moment,
    tenant_home,
    read_tenants,
    row_tenant,
):
    tenant_total = lax.axis_size("tenant")
    shard_count = lax.axis_size("fsdp")
    tenant_pos = lax.axis_index("tenant")
    device_pos = tenant_pos * shard_count + lax.axis_index("fsdp")
    position_count = adapters.shape[0]
    adapter_rank_size = adapters.shape[1]
    section_width = adapters.shape[2]
    hidden_width = tokens.shape[1]
    key_value_width = cotangent.shape[1]
    consumer_count = read_tenants.shape[0]
    fetch_count = read_tenants.shape[1]
    tenants_per_owner = fetch_count // tenant_total
    tenant_count = tenant_home.shape[0]
    adapter_scale = 2.0 / math.sqrt(hidden_width * adapter_rank_size)
    matches = read_tenants[:, :, None] == jnp.arange(tenant_count, dtype=jnp.int32)[None, None, :]
    home_slots = jnp.sum(jnp.where(matches, tenant_home[None, None, :], 0), axis=2)
    local_slot = home_slots % position_count
    wanted = lax.dynamic_slice_in_dim(
        local_slot, tenant_pos * tenants_per_owner, tenants_per_owner, 1
    )
    wanted = wanted.reshape(consumer_count * tenants_per_owner)
    selected_rows = jnp.take(adapters, wanted, axis=0).astype(jnp.bfloat16)
    fetched_copy = bring_back(selected_rows, tenant_total, shard_count, tenants_per_owner)
    down_matrix_rows = fetched_copy[:, :, :hidden_width].reshape(
        fetch_count * adapter_rank_size, hidden_width
    )
    up_matrix_rows = fetched_copy[:, :, hidden_width:].reshape(
        fetch_count * adapter_rank_size, key_value_width
    )
    read_block = lax.dynamic_slice_in_dim(read_tenants, device_pos, 1, 0)[0]
    selected_tenants = (row_tenant[:, None] == read_block[None, :]).astype(jnp.float32)
    selected_tenants = jnp.repeat(selected_tenants, adapter_rank_size, axis=1)
    contract_last = (((1,), (1,)), ((), ()))
    contract_first = (((0,), (0,)), ((), ()))
    low_all = lax.dot_general(
        tokens, down_matrix_rows, contract_last, preferred_element_type=jnp.float32
    )
    narrow_product = (low_all * selected_tenants).astype(jnp.bfloat16)
    frozen_output = jnp.dot(
        tokens,
        lax.all_gather(value_weight, "fsdp", axis=0, tiled=True),
        preferred_element_type=jnp.float32,
    )
    values = (
        frozen_output
        + adapter_scale
        * jnp.dot(narrow_product, up_matrix_rows, preferred_element_type=jnp.float32)
    ).astype(jnp.bfloat16)
    narrow_gradient = (
        adapter_scale
        * lax.dot_general(
            cotangent, up_matrix_rows, contract_last, preferred_element_type=jnp.float32
        )
        * selected_tenants
    ).astype(jnp.bfloat16)
    back_base = lax.dot_general(
        cotangent,
        lax.all_gather(value_weight, "fsdp", axis=0, tiled=True),
        contract_last,
        preferred_element_type=jnp.float32,
    )
    token_grad = (
        back_base + jnp.dot(narrow_gradient, down_matrix_rows, preferred_element_type=jnp.float32)
    ).astype(jnp.bfloat16)
    grad_down = lax.dot_general(
        narrow_gradient, tokens, contract_first, preferred_element_type=jnp.float32
    )
    up_gradient = adapter_scale * lax.dot_general(
        narrow_product, cotangent, contract_first, preferred_element_type=jnp.float32
    )
    fetched_gradient = jnp.concatenate([grad_down, up_gradient], axis=1).reshape(
        fetch_count, adapter_rank_size, shard_count * section_width
    )
    departing_rows = fetched_gradient.reshape(
        tenant_total, tenants_per_owner, adapter_rank_size, shard_count, section_width
    ).transpose(0, 3, 1, 2, 4)
    departing_rows = departing_rows.reshape(
        tenant_total * shard_count * tenants_per_owner, adapter_rank_size, section_width
    )
    received_rows = lax.all_to_all(
        departing_rows.astype(jnp.bfloat16),
        ("tenant", "fsdp"),
        split_axis=0,
        concat_axis=0,
        tiled=True,
    ).astype(departing_rows.dtype)
    received_rows = received_rows.reshape(
        consumer_count * tenants_per_owner, adapter_rank_size * section_width
    )
    one_hot = (wanted[:, None] == jnp.arange(position_count, dtype=jnp.int32)[None, :]).astype(
        jnp.float32
    )
    position_gradient = jnp.dot(
        one_hot.T,
        received_rows,
        precision=lax.Precision.HIGHEST,
        preferred_element_type=jnp.float32,
    )
    position_gradient = position_gradient.reshape(position_count, adapter_rank_size, section_width)
    new_first = beta_first * first_moment + (1.0 - beta_first) * position_gradient
    new_second = (
        beta_second * second_moment + (1.0 - beta_second) * position_gradient * position_gradient
    )
    new_adapters = adapters - learn_rate * (new_first / corr_first) / (
        jnp.sqrt(new_second / corr_second) + adam_eps
    )
    fresh_pick = jnp.take(new_adapters, wanted, axis=0).astype(jnp.bfloat16)
    refreshed = bring_back(fresh_pick, tenant_total, shard_count, tenants_per_owner)
    return (values, token_grad, new_adapters, new_first, new_second, refreshed)


def solution(mesh):
    return jax.shard_map(
        per_device,
        mesh=mesh,
        in_specs=(
            P(("tenant", "fsdp"), None),
            P(("tenant", "fsdp"), None),
            P("fsdp", None),
            P("tenant", None, "fsdp"),
            P("tenant", None, "fsdp"),
            P("tenant", None, "fsdp"),
            P(),
            P(),
            P(("tenant", "fsdp")),
        ),
        out_specs=(
            P(("tenant", "fsdp"), None),
            P(("tenant", "fsdp"), None),
            P("tenant", None, "fsdp"),
            P("tenant", None, "fsdp"),
            P("tenant", None, "fsdp"),
            P(("tenant", "fsdp"), None, None),
        ),
        check_vma=False,
    )
```

profile of v0, /device:TPU:0, one launch (start us, length us, event | category | flops | bytes accessed | tf_op | source)
XLA Modules:
  0.0 356.1 jit_solution(11708247615714546399)
XLA Ops:
  7.2 0.0 copy-start
  7.2 0.0 copy-start.8
  7.2 0.0 copy-start.10
  7.2 0.0 copy-start.4
  7.2 0.0 all-gather.2.cloned.1.call-start
  7.3 0.7 all-gather.2.cloned.1.call-update
  8.0 0.2 select_reduce_fusion
  8.3 0.3 copy-done.4
  8.6 0.7 gather_fusion
  9.3 1.3 select_convert_fusion.1
  10.6 7.3 %all-to-all-start = ((bf16[32,16,1152]{2,1,0:T(8,128)(2,1)}), bf16[32,16,1152]{2,1,0:T(8,128)(2,1)S(1)}, u32[]{:S(2)}, u32[]{:S(2)}) async-start(bf16[32,16,1152]{2,1,0:T(8,128)(2,1)} %select_convert_fusion.1), calls=%async_computation | async-start | bytes 2359296 | tf_op jit(solution)/shard_map/all_to_all | solution.py:19
  17.9 0.2 dynamic-slice_reduce_fusion
  18.1 0.1 compare_convert_fusion
  18.2 53.1 %all-to-all-done = bf16[32,16,1152]{2,1,0:T(8,128)(2,1)S(1)} async-done(((bf16[32,16,1152]{2,1,0:T(8,128)(2,1)}), bf16[32,16,1152]{2,1,0:T(8,128)(2,1)S(1)}, u32[]{:S(2)}, u32[]{:S(2)}) %all-to-all-start) | async-done | bytes 1179680 | tf_op jit(solution)/shard_map/all_to_all | solution.py:19
  71.3 1.2 copy.68
  72.5 1.6 reshape.54
  74.2 0.1 slice.12
  74.3 6.1 %fusion.9 = bf16[512,64]{0,1:T(8,128)(2,1)S(1)} fusion(f32[512,64]{0,1:T(8,128)S(1)} %bitcast.82, bf16[64,8192]{1,0:T(8,128)(2,1)S(1)} %bitcast.74, bf16[512,8192]{1,0:T(8,128)(2,1)} %param.11), kind=kOutput, calls=%fused_computation.25 | convolution fusion | flops 536936448 | bytes 9633792 | tf_op jit(solution)/shard_map/dot_general | solution.py:76
  80.4 0.3 fusion.5
  80.7 0.4 fusion.10
  81.2 5.0 %convolution_convert_fusion = bf16[64,8192]{1,0:T(8,128)(2,1)S(1)} fusion(bf16[512,64]{0,1:T(8,128)(2,1)S(1)} %fusion.10, bf16[512,8192]{1,0:T(8,128)(2,1)} %param.11), kind=kOutput, calls=%fused_computation.3 | convolution fusion | flops 537395200 | bytes 9502720 | tf_op jit(solution)/shard_map/dot_general | solution.py:106
  86.2 0.1 pad_maximum_fusion
  86.3 0.2 copy.47
  86.5 0.0 copy-start.12
  86.5 0.1 copy.37
  86.7 0.0 copy-start.5
  86.7 0.0 copy-start.11
  86.7 54.8 %all_to_all.15 = bf16[32,16,1152]{2,1,0:T(8,128)(2,1)S(1)} all-to-all(bf16[32,16,1152]{2,1,0:T(8,128)(2,1)S(1)} %bitcast.81), channel_id=1, replica_groups=mesh['tenant'=4,'fsdp'=8] {'tenant','fsdp'}, dimensions={0} | all-to-all | bytes 2359296 | tf_op jit(solution)/shard_map/all_to_all | solution.py:121
  141.5 0.0 copy-done.5
  141.5 3.2 copy_subtract_fusion
  144.7 0.4 copy.43
  145.1 0.0 copy-start.2
  145.1 1.7 gather_fusion.1
  146.8 2.7 select_convert_fusion
  149.4 2.8 all-to-all-start.2
  152.3 0.0 copy-start.7
  152.3 1.8 fusion.17
  154.1 1.4 copy.44
  155.5 1.4 copy.45
  156.8 61.2 %all-to-all-done.2 = bf16[32,16,1152]{2,1,0:T(8,128)(2,1)S(1)} async-done(((bf16[32,16,1152]{2,1,0:T(8,128)(2,1)}), bf16[32,16,1152]{2,1,0:T(8,128)(2,1)S(1)}, u32[]{:S(2)}, u32[]{:S(2)}) %all-to-all-start.2) | async-done | bytes 1179680 | tf_op jit(solution)/shard_map/all_to_all | solution.py:19
  218.0 1.2 copy.42
  219.2 2.4 reshape.60
  221.7 84.6 %all-gather.2.cloned.1.call-done = bf16[8192,1024]{1,0:T(8,128)(2,1)} async-done(((bf16[1024,1024]{1,0:T(8,128)(2,1)}), bf16[8192,1024]{1,0:T(8,128)(2,1)}) %all-gather.2.cloned.1.call-update) | async-done | bytes 16777232 | tf_op jit(solution)/shard_map/all_gather | solution.py:82
  306.3 15.7 %fusion.18 = f32[512,8192]{1,0:T(8,128)} fusion(bf16[512,1024]{1,0:T(8,128)(2,1)S(1)} %copy-done, bf16[8192,1024]{1,0:T(8,128)(2,1)} %all-gather.2.cloned.1.call-done), kind=kOutput, calls=%fused_computation.44 | convolution fusion | flops 8589934592 | bytes 34603008 | tf_op jit(solution)/shard_map/dot_general | solution.py:97
  322.0 11.7 %add_convert_fusion = bf16[512,8192]{1,0:T(8,128)(2,1)} fusion(f32[512,8192]{1,0:T(8,128)} %fusion.18, bf16[512,64]{0,1:T(8,128)(2,1)S(1)} %fusion.10, bf16[64,8192]{1,0:T(8,128)(2,1)S(1)} %bitcast.75), kind=kOutput, calls=%fused_computation.2 | convolution fusion | flops 545259520 | bytes 26279936 | tf_op jit(solution)/shard_map/dot_general | solution.py:104
  333.6 0.0 copy-done.3
  333.6 15.6 %add_convert_fusion.1 = bf16[512,1024]{1,0:T(8,128)(2,1)} fusion(f32[512,1024]{1,0:T(8,128)S(1)} %copy-done.3, bf16[512,8192]{1,0:T(8,128)(2,1)} %param.11, bf16[8192,1024]{1,0:T(8,128)(2,1)} %all-gather.2.cloned.1.call-done), kind=kOutput, calls=%fused_computation.6 | convolution fusion | flops 8591507456 | bytes 28311552 | tf_op jit(solution)/shard_map/dot_general | solution.py:80
  349.3 0.0 copy-done.1
  (19 shorter events, 0.1 us)
Async XLA Ops:
  7.2 73.3 %copy-start = (bf16[512,1024]{1,0:T(8,128)(2,1)S(1)}, bf16[512,1024]{1,0:T(8,128)(2,1)}, u32[]{:S(2)}) copy-start(bf16[512,1024]{1,0:T(8,128)(2,1)} %param.12) | copy-start | bytes 3145732
  7.2 0.8 copy-start.8
  7.2 0.8 copy-start.10
  7.2 1.4 copy-start.4
  7.2 299.0 %all-gather.2.cloned.1.call-start = ((), (), s32[]{:S(2)}) async-start(), calls=%async_computation.3 | async-start | bytes 18874368 | tf_op jit(solution)/shard_map/all_gather | solution.py:82
  10.6 7.5 %copy-start.9 = (s32[512]{0:T(512)S(1)}, s32[512]{0:T(512)}, u32[]{:S(2)}) copy-start(s32[512]{0:T(512)} %param.19) | copy-start | bytes 6148
  10.6 60.7 %all-to-all-start = ((bf16[32,16,1152]{2,1,0:T(8,128)(2,1)}), bf16[32,16,1152]{2,1,0:T(8,128)(2,1)S(1)}, u32[]{:S(2)}, u32[]{:S(2)}) async-start(bf16[32,16,1152]{2,1,0:T(8,128)(2,1)} %select_convert_fusion.1), calls=%async_computation | async-start | bytes 2359296 | tf_op jit(solution)/shard_map/all_to_all | solution.py:19
  86.5 55.0 %copy-start.12 = (f32[16,16,1152]{2,1,0:T(8,128)S(1)}, f32[16,16,1152]{2,1,0:T(8,128)}, u32[]{:S(2)}) copy-start(f32[16,16,1152]{2,1,0:T(8,128)} %param.16) | copy-start | bytes 3538948
  86.7 54.8 %copy-start.5 = (f32[16,16,1152]{2,1,0:T(8,128)S(1)}, f32[16,16,1152]{2,1,0:T(8,128)}, u32[]{:S(2)}) copy-start(f32[16,16,1152]{2,1,0:T(8,128)} %param.14) | copy-start | bytes 3538948
  86.7 54.8 %copy-start.11 = (f32[16,16,1152]{2,1,0:T(8,128)S(1)}, f32[16,16,1152]{2,1,0:T(8,128)}, u32[]{:S(2)}) copy-start(f32[16,16,1152]{2,1,0:T(8,128)} %param.15) | copy-start | bytes 3538948
  145.1 1.7 copy-start.2
  149.4 68.6 %all-to-all-start.2 = ((bf16[32,16,1152]{2,1,0:T(8,128)(2,1)}), bf16[32,16,1152]{2,1,0:T(8,128)(2,1)S(1)}, u32[]{:S(2)}, u32[]{:S(2)}) async-start(bf16[32,16,1152]{2,1,0:T(8,128)(2,1)} %select_convert_fusion), calls=%async_computation.2 | async-start | bytes 2359296 | tf_op jit(solution)/shard_map/all_to_all | solution.py:19
  152.3 1.8 copy-start.7
  154.1 1.4 copy-start.6
  322.0 11.7 %copy-start.3 = (f32[512,1024]{1,0:T(8,128)S(1)}, f32[512,1024]{1,0:T(8,128)}, u32[]{:S(2)}) copy-start(f32[512,1024]{1,0:T(8,128)} %fusion.17) | copy-start | bytes 6291460
  333.6 15.6 %copy-start.1 = (bf16[512,1024]{1,0:T(8,128)(2,1)S(1)}, bf16[512,1024]{1,0:T(8,128)(2,1)}, u32[]{:S(2)}) copy-start(bf16[512,1024]{1,0:T(8,128)(2,1)} %param.12) | copy-start | bytes 3145732
Sparse Core Ops, SparseCore 0:
  10.1 296.0 all-gather.1
where the time goes:
time: 357 us; the launch traced here: 356 us
  waiting for transfers between devices  200 us (56%)
  matrix products  59.9 us (17%)
  blocking collectives  54.8 us (15%)
  between operations  14.3 us (4%)
  local copies, waits for them, and re-layouts  13 us (4%)
  starting transfers between devices  10.2 us (3%)
  other arithmetic  4.35 us (1%)
    all_to_all x2, waiting for transfers between devices, bring_back(): lax.all_to_all(selected_rows, ('tenant', 'fsdp'), split_axis=0, concat_ax...  114 us
    all_gather x1, waiting for transfers between devices, per_device(): lax.all_gather(value_weight, 'fsdp', axis=0, tiled=True)  84.6 us
    all_to_all x1, blocking collectives, per_device(): lax.all_to_all(departing_rows.astype(jnp.bfloat16), ('tenant', 'fsdp'), s...  54.8 us
    dot_general x1, matrix products, per_device(): lax.dot_general(cotangent, lax.all_gather(value_weight, 'fsdp', axis=0, t...  15.7 us
    dot_general x1, matrix products, per_device(): jnp.dot(tokens, lax.all_gather(value_weight, 'fsdp', axis=0, tiled=True),...  15.6 us
    dot_general x1, matrix products, per_device(): jnp.dot(narrow_gradient, down_matrix_rows, preferred_element_type=jnp.flo...  11.7 us
    all_to_all x2, starting transfers between devices, bring_back(): lax.all_to_all(selected_rows, ('tenant', 'fsdp'), split_axis=0, concat_ax...  10.2 us
  transfers between devices with their start and end apart: 3, of which 3 were waited for; matrix products, arithmetic and copies ran while one was open for 10% of the time, Pallas kernels for 0%

commit v1 on v0

--- a/solution.py
+++ b/solution.py
@@ -1,8 +1,11 @@
+import functools
 import math
 
 import jax
 import jax.numpy as jnp
 from jax import lax
+from jax.experimental import pallas as pl
+from jax.experimental.pallas import tpu as pltpu
 from jax.sharding import PartitionSpec as P
 
 beta_first = 0.9
@@ -150,9 +153,450 @@
     return (values, token_grad, new_adapters, new_first, new_second, refreshed)
 
 
+MESH = pl.DeviceIdType.MESH
+
+
+def step_kernel(
+    T, F, scale,
+    pick, mask, adapters, w_hbm, tok_hbm, cot_hbm, mom1_hbm, mom2_hbm,
+    values, tg_hbm, new_ad, new_m1, new_m2, refreshed,
+    wbuf, tokens, cot, mom1, mom2, sel, asm, grads, got, acc, low, tgbuf,
+    load_sem, ag_send, ag_recv, a2a_send, a2a_recv, tg_sem,
+):
+    t = lax.axis_index("tenant")
+    f = lax.axis_index("fsdp")
+    D = T * F
+    Z = F // 2
+    R = asm.shape[0] // T
+    SW = sel.shape[1]
+    shard = wbuf.shape[1]
+    QR = shard // T
+    KV = wbuf.shape[2]
+    width = tokens.shape[1]
+    me = t * F + f
+    z, y = f // 2, f % 2
+    oy = 1 - y
+    half = T // 2
+    tx = (t + half) % T
+    tc = t + 1 - 2 * (t % 2)
+    qx = tx
+
+    loads = [
+        pltpu.make_async_copy(w_hbm, wbuf.at[f], load_sem.at[0]),
+        pltpu.make_async_copy(tok_hbm, tokens, load_sem.at[1]),
+        pltpu.make_async_copy(cot_hbm, cot, load_sem.at[2]),
+        pltpu.make_async_copy(mom1_hbm, mom1, load_sem.at[3]),
+        pltpu.make_async_copy(mom2_hbm, mom2, load_sem.at[4]),
+    ]
+    loads[0].start()
+    loads[1].start()
+    loads[2].start()
+    loads[3].start()
+    loads[4].start()
+    barrier = pltpu.get_barrier_semaphore()
+
+    def greet(k, carry):
+        dev = (me + k) % D
+        pl.semaphore_signal(
+            barrier, inc=1, device_id=(dev // F, dev % F), device_id_type=MESH
+        )
+        return carry
+
+    lax.fori_loop(1, D, greet, 0)
+
+    sel[...] = jnp.dot(
+        pick[...], adapters[...].astype(jnp.bfloat16), preferred_element_type=jnp.float32
+    ).astype(jnp.bfloat16)
+    loads[0].wait()
+    pl.semaphore_wait(barrier, D - 1)
+
+    def piece(shard_id, q):
+        return wbuf.at[shard_id, pl.ds(pl.multiple_of(q * QR, QR), QR)]
+
+    def ag(kind, shard_id, q, dst_t, dst_f):
+        return pltpu.make_async_remote_copy(
+            src_ref=piece(shard_id, q),
+            dst_ref=piece(shard_id, q),
+            send_sem=ag_send.at[kind, shard_id],
+            recv_sem=ag_recv.at[shard_id, q],
+            device_id=(dst_t, dst_f),
+            device_id_type=MESH,
+        )
+
+    def arrive(shard_id, q):
+        pltpu.make_async_copy(
+            piece(shard_id, q), piece(shard_id, q), ag_recv.at[shard_id, q]
+        ).wait()
+
+    def z_own(act):
+        @pl.when(z + 1 < Z)
+        def _():
+            act(ag(0, f, t, t, f + 2))
+
+        @pl.when(z > 0)
+        def _():
+            act(ag(1, f, t, t, f - 2))
+
+    def y_own(act):
+        act(ag(2, f, t, t, z * 2 + oy))
+        act(ag(3, f, qx, t, z * 2 + oy))
+
+    orders = [
+        sorted(range(Z), key=lambda s, at=at: (abs(s - at), s if at < Z // 2 else -s))
+        for at in range(Z)
+    ]
+
+    def near(i):
+        pos = 0
+        for at in range(Z):
+            pos = jnp.where(z == at, orders[at][i], pos)
+        return pos
+
+    zz = [z] + [near(i) for i in range(1, Z)]
+
+    def e1(i, act, wait):
+        s = zz[i] * 2 + y
+        if wait:
+            arrive(s, t)
+
+        @pl.when(jnp.logical_and(zz[i] < z, z + 1 < Z))
+        def _():
+            act(ag(0, s, t, t, f + 2))
+
+        @pl.when(jnp.logical_and(zz[i] > z, z > 0))
+        def _():
+            act(ag(1, s, t, t, f - 2))
+
+        act(ag(4, s, t, tx, f))
+        act(ag(2, s, t, t, z * 2 + oy))
+        act(ag(5, s, t, tc, f))
+
+    def e2own(act, wait):
+        s = z * 2 + oy
+        if wait:
+            arrive(s, t)
+            arrive(s, qx)
+        act(ag(5, s, t, tc, f))
+        act(ag(6, s, qx, tc, f))
+
+    def e2(i, act, wait):
+        s = zz[i] * 2 + oy
+        if wait:
+            arrive(s, t)
+        act(ag(4, s, t, tx, f))
+        act(ag(5, s, t, tc, f))
+
+    def e3(i, yy, act, wait):
+        s = zz[i] * 2 + yy
+        if wait:
+            arrive(s, qx)
+        act(ag(6, s, qx, tc, f))
+
+    def start(copy):
+        copy.start()
+
+    def sent(copy):
+        copy.wait_send()
+
+    def rows(i):
+        return pl.ds(pl.multiple_of(i * R, R), R)
+
+    def cols(i):
+        return pl.ds(pl.multiple_of(i * SW, SW), SW)
+
+    def spread(n, src_of, dst_at):
+        def go(k, carry):
+            dev = (me + k) % D
+            pltpu.make_async_remote_copy(
+                src_ref=src_of(dev),
+                dst_ref=dst_at,
+                send_sem=a2a_send.at[n, dev],
+                recv_sem=a2a_recv.at[n, me],
+                device_id=(dev // F, dev % F),
+                device_id_type=MESH,
+            ).start()
+            return carry
+
+        lax.fori_loop(1, D, go, 0)
+        pltpu.make_async_copy(src_of(me), dst_at, a2a_recv.at[n, me]).start()
+
+    def collect(n, dst_of):
+        def go(k, carry):
+            dst = dst_of(k)
+            pltpu.make_async_copy(dst, dst, a2a_recv.at[n, k]).wait()
+            return carry
+
+        lax.fori_loop(0, D, go, 0)
+
+    def drain(n, src_of):
+        def go(k, carry):
+            dev = (me + k) % D
+            pltpu.make_async_remote_copy(
+                src_ref=src_of(dev),
+                dst_ref=src_of(dev),
+                send_sem=a2a_send.at[n, dev],
+                recv_sem=a2a_recv.at[n, me],
+                device_id=(dev // F, dev % F),
+                device_id_type=MESH,
+            ).wait_send()
+            return carry
+
+        lax.fori_loop(1, D, go, 0)
+
+    def sel_of(dev):
+        return sel.at[rows(dev)]
+
+    def asm_of(dev):
+        return asm.at[rows(dev // F), cols(dev % F)]
+
+    def grad_of(dev):
+        return grads.at[rows(dev // F), cols(dev % F)]
+
+    def got_of(dev):
+        return got.at[rows(dev)]
+
+    def ref_of(dev):
+        return refreshed.at[rows(dev // F), cols(dev % F)]
+
+    last = (((1,), (1,)), ((), ()))
+    first = (((0,), (0,)), ((), ()))
+
+    def wide(i):
+        return pl.ds(pl.multiple_of(i * shard, shard), shard)
+
+    z_own(start)
+    y_own(start)
+    spread(0, sel_of, asm_of(me))
+    for n in range(1, 5):
+        loads[n].wait()
+    e1(1, start, True)
+    e2own(start, True)
+    collect(0, asm_of)
+
+    low[...] = jnp.zeros_like(low)
+
+    def lower(k, carry):
+        low[...] += lax.dot_general(
+            tokens[:, wide(k)], asm[:, wide(k)], last, preferred_element_type=jnp.float32
+        )
+        return carry
+
+    ups = pl.ds(width, KV)
+    narrow_gradient = (
+        scale
+        * lax.dot_general(cot[...], asm[:, ups], last, preferred_element_type=jnp.float32)
+        * mask[...]
+    )
+    ng = narrow_gradient.astype(jnp.bfloat16)
+    ng_t = ng.astype(jnp.float32).T.astype(jnp.bfloat16)
+
+    def gradient(k, carry):
+        grads[:, wide(k)] = jnp.dot(
+            ng_t, tokens[:, wide(k)], preferred_element_type=jnp.float32
+        ).astype(jnp.bfloat16)
+        return carry
+
+    lax.fori_loop(0, F, gradient, 0)
+    lax.fori_loop(0, F, lower, 0)
+    nprod = (low[...] * mask[...]).astype(jnp.bfloat16)
+    np_t = nprod.astype(jnp.float32).T.astype(jnp.bfloat16)
+    grads[:, ups] = (
+        scale * jnp.dot(np_t, cot[...], preferred_element_type=jnp.float32)
+    ).astype(jnp.bfloat16)
+    spread(1, grad_of, got_of(me))
+    if Z > 2:
+        e1(2, start, True)
+    low[...] = ng.astype(jnp.float32)
+    acc[...] = scale * jnp.dot(nprod, asm[:, ups], preferred_element_type=jnp.float32)
+
+    def tg_copy(n, s):
+        return pltpu.make_async_copy(
+            tgbuf.at[n % 2], tg_hbm.at[:, wide(s)], tg_sem.at[n % 2]
+        )
+
+    done = []
+
+    def dots(i, yy):
+        s = zz[i] * 2 + yy
+        n = len(done)
+        if i == 0 and n > 0:
+            arrive(s, tc)
+            arrive(s, (tc + half) % T)
+        elif i > 0:
+            arrive(s, tc)
+            arrive(s, (tc + half) % T)
+        if n >= 2:
+            tg_copy(n, done[n - 2]).wait()
+
+        def fwd(k, carry):
+            block = pl.ds(pl.multiple_of(k * QR, QR), QR)
+            acc[:, block] += jnp.dot(
+                tokens[:, wide(s)], wbuf[s, :, block], preferred_element_type=jnp.float32
+            )
+            return carry
+
+        def bwd(k, carry):
+            block = pl.ds(pl.multiple_of(k * QR, QR), QR)
+            here = pl.ds(pl.multiple_of(s * shard + k * QR, QR), QR)
+            out = lax.dot_general(
+                cot[...], wbuf[s, block, :], last, preferred_element_type=jnp.float32
+            )
+            out += jnp.dot(
+                low[...].astype(jnp.bfloat16), asm[:, here],
+                preferred_element_type=jnp.float32,
+            )
+            tgbuf[n % 2, :, block] = out.astype(jnp.bfloat16)
+            return carry
+
+        lax.fori_loop(0, KV // QR, fwd, 0)
+        lax.fori_loop(0, T, bwd, 0)
+        tg_copy(n, s).start()
+        done.append(s)
+
+    def update():
+        collect(1, got_of)
+        g = lax.dot_general(pick[...], got[...], first, preferred_element_type=jnp.float32)
+        m1 = beta_first * mom1[...] + (1.0 - beta_first) * g
+        m2 = beta_second * mom2[...] + (1.0 - beta_second) * g * g
+        new_m1[...] = m1
+        new_m2[...] = m2
+        na = adapters[...] - learn_rate * (m1 / corr_first) / (
+            jnp.sqrt(m2 / corr_second) + adam_eps
+        )
+        new_ad[...] = na
+        drain(0, sel_of)
+        sel[...] = jnp.dot(
+            pick[...], na.astype(jnp.bfloat16), preferred_element_type=jnp.float32
+        ).astype(jnp.bfloat16)
+        spread(2, sel_of, ref_of(me))
+
+    dots(0, y)
+    e2(1, start, True)
+    for i in range(3, Z):
+        e1(i, start, True)
+    e3(1, y, start, True)
+    dots(0, oy)
+    for i in range(2, Z):
+        e2(i, start, True)
+        e3(i - 1, oy, start, True)
+        e3(i, y, start, True)
+        dots(i - 1, y)
+        if i < Z - 1:
+            dots(i - 1, oy)
+    e3(Z - 1, oy, start, True)
+    update()
+    dots(Z - 2, oy)
+    dots(Z - 1, y)
+    dots(Z - 1, oy)
+    values[...] = acc[...].astype(jnp.bfloat16)
+    collect(2, ref_of)
+    for n in (len(done) - 2, len(done) - 1):
+        tg_copy(n, done[n]).wait()
+    drain(1, grad_of)
+    drain(2, sel_of)
+    z_own(sent)
+    y_own(sent)
+    e2own(sent, False)
+    for i in range(1, Z):
+        e1(i, sent, False)
+        e2(i, sent, False)
+        e3(i, y, sent, False)
+        e3(i, oy, sent, False)
+
+
+def kernel_device(
+    tokens, cotangent, value_weight, adapters, first_moment, second_moment,
+    tenant_home, read_tenants, row_tenant,
+):
+    T = lax.axis_size("tenant")
+    F = lax.axis_size("fsdp")
+    D = T * F
+    tenant_pos = lax.axis_index("tenant")
+    device_pos = tenant_pos * F + lax.axis_index("fsdp")
+    slots, rank, sw = adapters.shape
+    width = tokens.shape[1]
+    kv = cotangent.shape[1]
+    rows = tokens.shape[0]
+    scale = 2.0 / math.sqrt(width * rank)
+    tenant_count = tenant_home.shape[0]
+    mine = lax.dynamic_slice_in_dim(read_tenants, tenant_pos, 1, 1)[:, 0]
+    hits = mine[:, None] == jnp.arange(tenant_count, dtype=jnp.int32)[None, :]
+    wanted = jnp.sum(jnp.where(hits, tenant_home[None, :], 0), axis=1) % slots
+    left = jnp.arange(D * rank, dtype=jnp.int32)
+    right = jnp.arange(slots * rank, dtype=jnp.int32)
+    goal = jnp.repeat(wanted, rank) * rank + left % rank
+    pick = (goal[:, None] == right[None, :]).astype(jnp.bfloat16)
+    read_block = lax.dynamic_slice_in_dim(read_tenants, device_pos, 1, 0)[0]
+    mask = row_tenant[:, None] == jnp.repeat(read_block, rank)[None, :]
+    mask = mask.astype(jnp.float32)
+    flat = (slots * rank, sw)
+    f32, bf16 = jnp.float32, jnp.bfloat16
+    vmem = pl.BlockSpec(memory_space=pltpu.VMEM)
+    hbm = pl.BlockSpec(memory_space=pl.ANY)
+    dma = pltpu.SemaphoreType.DMA
+    values, token_grad, new_ad, new_m1, new_m2, refreshed = pl.pallas_call(
+        functools.partial(step_kernel, T, F, scale),
+        out_shape=(
+            jax.ShapeDtypeStruct((rows, kv), bf16),
+            jax.ShapeDtypeStruct((rows, width), bf16),
+            jax.ShapeDtypeStruct(flat, f32),
+            jax.ShapeDtypeStruct(flat, f32),
+            jax.ShapeDtypeStruct(flat, f32),
+            jax.ShapeDtypeStruct((T * rank, F * sw), bf16),
+        ),
+        in_specs=[vmem, vmem, vmem, hbm, hbm, hbm, hbm, hbm],
+        out_specs=(vmem, hbm, vmem, vmem, vmem, vmem),
+        scratch_shapes=[
+            pltpu.VMEM((F,) + value_weight.shape, bf16),
+            pltpu.VMEM(tokens.shape, bf16),
+            pltpu.VMEM(cotangent.shape, bf16),
+            pltpu.VMEM(flat, f32),
+            pltpu.VMEM(flat, f32),
+            pltpu.VMEM((D * rank, sw), bf16),
+            pltpu.VMEM((T * rank, F * sw), bf16),
+            pltpu.VMEM((T * rank, F * sw), bf16),
+            pltpu.VMEM((D * rank, sw), bf16),
+            pltpu.VMEM((rows, kv), f32),
+            pltpu.VMEM((rows, T * rank), f32),
+            pltpu.VMEM((2, rows, width // F), bf16),
+            dma((5,)),
+            dma((7, F)),
+            dma((F, T)),
+            dma((3, D)),
+            dma((3, D)),
+            dma((2,)),
+        ],
+        compiler_params=pltpu.CompilerParams(
+            collective_id=0, has_side_effects=True, vmem_limit_bytes=67043328
+        ),
+    )(
+        pick, mask, adapters.reshape(flat), value_weight, tokens, cotangent,
+        first_moment.reshape(flat), second_moment.reshape(flat),
+    )
+    shape = adapters.shape
+    return (
+        values, token_grad, new_ad.reshape(shape), new_m1.reshape(shape),
+        new_m2.reshape(shape), refreshed.reshape(T, rank, F * sw),
+    )
+
+
+def dispatch(*args):
+    T = lax.axis_size("tenant")
+    F = lax.axis_size("fsdp")
+    adapters, read_tenants = args[3], args[7]
+    fits = (
+        adapters.shape[2] % 128 == 0
+        and read_tenants.shape[1] == T
+        and T == 4
+        and F % 2 == 0
+        and F >= 6
+    )
+    return (kernel_device if fits else per_device)(*args)
+
+
 def solution(mesh):
     return jax.shard_map(
-        per_device,
+        dispatch,
         mesh=mesh,
         in_specs=(
             P(("tenant", "fsdp"), None),

time: 357 us -> 198 us (0.55)
  waiting for transfers between devices: 200 us -> 0 us
  Pallas kernels: 0 us -> 176 us
  matrix products: 59.9 us -> 0 us
  blocking collectives: 54.8 us -> 0 us
  between operations: 14.3 us -> 0.66 us
  starting transfers between devices: 10.2 us -> 0 us
  local copies, waits for them, and re-layouts: 13 us -> 18.1 us
    pallas_call x0 -> x1, Pallas kernels: none -> 176 us  [kernel_device(): pl.pallas_call(functools.partial(step_kernel, T, F, scale), out_shape=(ja...]
    all_to_all x2 -> x0, waiting for transfers between devices: 114 us -> none  [bring_back(): lax.all_to_all(selected_rows, ('tenant', 'fsdp'), split_axis=0, concat_ax...]
    all_gather x1 -> x0, waiting for transfers between devices: 84.6 us -> none  [per_device(): lax.all_gather(value_weight, 'fsdp', axis=0, tiled=True)]
    dot_general x9 -> x0, matrix products: 59.9 us -> none  [the longest x1 15.7 us: per_device(): lax.dot_general(cotangent, lax.all_gather(value_weight, 'fsdp', axis=0, t...]
    all_to_all x1 -> x0, blocking collectives: 54.8 us -> none  [per_device(): lax.all_to_all(departing_rows.astype(jnp.bfloat16), ('tenant', 'fsdp'), s...]
    unnamed x30 -> x14, local copies, waits for them, and re-layouts: 3.71 us -> 16.2 us
    all_to_all x2 -> x0, starting transfers between devices: 10.2 us -> none  [bring_back(): lax.all_to_all(selected_rows, ('tenant', 'fsdp'), split_axis=0, concat_ax...]
    reshape x3 -> x0, local copies, waits for them, and re-layouts: 5.29 us -> none  [the longest x2 4.06 us: bring_back(): received_rows.reshape(tenant_total * tenants_per_owner, adapter_rank_size...]
  transfers between devices with their start and end apart: 3 -> 0, of which waited for: 3 -> 0; matrix products, arithmetic and copies ran while one was open for 10% -> 0% of each run, Pallas kernels for 0% -> 0%
where the time goes in v1:
time: 198 us
  Pallas kernels  176 us (89%)
  local copies, waits for them, and re-layouts  18.1 us (9%)
  other arithmetic  3.22 us (2%)
    pallas_call x1, Pallas kernels, kernel_device(): pl.pallas_call(functools.partial(step_kernel, T, F, scale), out_shape=(ja...  176 us
    unnamed x14, local copies, waits for them, and re-layouts  16.2 us

profile of v1, /device:TPU:0, one launch (start us, length us, event | category | flops | bytes accessed | tf_op | source)
XLA Modules:
  0.0 197.6 jit_solution(8248960216971860528)
XLA Ops:
  0.6 0.9 dynamic-slice_reduce_fusion
  1.5 0.7 dynamic-slice_bitcast_fusion
  2.2 0.8 select_reduce_fusion
  3.0 0.1 broadcast_in_dim.26
  3.1 0.1 eq.55
  3.2 0.1 broadcast_in_dim.25
  3.3 0.1 mul.18
  3.4 0.8 fusion.pick
  4.2 1.5 compare_convert_fusion.mask
  5.7 175.6 %shard_map.136 = (bf16[512,1024]{1,0:T(8,128)(2,1)}, bf16[512,8192]{1,0:T(8,128)(2,1)}, f32[256,1152]{1,0:T(8,128)}, f32[256,1152]{1,0:T(8,128)}, f32[256,1152]{1,0:T(8,128)}, /*index=5*/bf16[64,9216]{1,0:T(8,128)(2,1)}) custom-call(bf16[512,256]{1,0:T(8,128)(2,1)} %fusion.pick, f32[512,64]{1,0:T(8,128)} %compare_convert_fusion.mask, f32[256,1152]{1,0:T(8,128)} %bitcast.13, ...), custom_call_target="tpu_custom_call" | custom-call | tf_op jit(solution)/shard_map/pallas_call | solution.py:537
  181.4 2.3 %copy.21 = bf16[512,1024]{1,0:T(8,128)(2,1)} copy(bf16[512,1024]{1,0:T(8,128)(2,1)} %get-tuple-element.24) | data formatting | bytes 2097152
  183.6 0.0 copy-start.3
  183.6 7.9 %copy.22 = bf16[512,8192]{1,0:T(8,128)(2,1)} copy(bf16[512,8192]{1,0:T(8,128)(2,1)} %get-tuple-element.25) | data formatting | bytes 16777216
  191.5 0.0 copy-done.3
  191.5 0.0 copy-start.2
  191.5 1.0 copy.23
  192.5 0.7 copy-done.2
  193.2 0.0 copy-start.1
  193.2 1.0 copy.24
  194.2 0.7 copy-done.1
  194.9 0.0 copy-start
  194.9 1.0 copy.25
  195.9 0.7 copy-done
  196.6 1.0 copy.26
  (2 shorter events, 0.0 us)
Async XLA Ops:
  183.6 7.9 %copy-start.3 = (f32[256,1152]{1,0:T(8,128)S(1)}, f32[256,1152]{1,0:T(8,128)}, u32[]{:S(2)}) copy-start(f32[256,1152]{1,0:T(8,128)} %get-tuple-element.14) | copy-start | bytes 3538948
  191.5 1.7 copy-start.2
  193.2 1.7 copy-start.1
  194.9 1.7 copy-start

commit v2 on v1

--- a/solution.py
+++ b/solution.py
@@ -159,7 +159,7 @@
 def step_kernel(
     T, F, scale,
     pick, mask, adapters, w_hbm, tok_hbm, cot_hbm, mom1_hbm, mom2_hbm,
-    values, tg_hbm, new_ad, new_m1, new_m2, refreshed,
+    values, tg_hbm, slot_grad, refreshed,
     wbuf, tokens, cot, mom1, mom2, sel, asm, grads, got, acc, low, tgbuf,
     load_sem, ag_send, ag_recv, a2a_send, a2a_recv, tg_sem,
 ):
@@ -239,6 +239,8 @@
 
     def y_own(act):
         act(ag(2, f, t, t, z * 2 + oy))
+
+    def y_more(act):
         act(ag(3, f, qx, t, z * 2 + oy))
 
     orders = [
@@ -366,11 +368,16 @@
 
     z_own(start)
     y_own(start)
-    spread(0, sel_of, asm_of(me))
     for n in range(1, 5):
         loads[n].wait()
     e1(1, start, True)
+    spread(0, sel_of, asm_of(me))
+    y_more(start)
+    e1(2, start, True)
     e2own(start, True)
+    e2(1, start, True)
+    for i in range(3, Z):
+        e1(i, start, True)
     collect(0, asm_of)
 
     low[...] = jnp.zeros_like(low)
@@ -404,8 +411,6 @@
         scale * jnp.dot(np_t, cot[...], preferred_element_type=jnp.float32)
     ).astype(jnp.bfloat16)
     spread(1, grad_of, got_of(me))
-    if Z > 2:
-        e1(2, start, True)
     low[...] = ng.astype(jnp.float32)
     acc[...] = scale * jnp.dot(nprod, asm[:, ups], preferred_element_type=jnp.float32)
 
@@ -458,12 +463,10 @@
         g = lax.dot_general(pick[...], got[...], first, preferred_element_type=jnp.float32)
         m1 = beta_first * mom1[...] + (1.0 - beta_first) * g
         m2 = beta_second * mom2[...] + (1.0 - beta_second) * g * g
-        new_m1[...] = m1
-        new_m2[...] = m2
         na = adapters[...] - learn_rate * (m1 / corr_first) / (
             jnp.sqrt(m2 / corr_second) + adam_eps
         )
-        new_ad[...] = na
+        slot_grad[...] = g
         drain(0, sel_of)
         sel[...] = jnp.dot(
             pick[...], na.astype(jnp.bfloat16), preferred_element_type=jnp.float32
@@ -471,9 +474,6 @@
         spread(2, sel_of, ref_of(me))
 
     dots(0, y)
-    e2(1, start, True)
-    for i in range(3, Z):
-        e1(i, start, True)
     e3(1, y, start, True)
     dots(0, oy)
     for i in range(2, Z):
@@ -496,6 +496,7 @@
     drain(2, sel_of)
     z_own(sent)
     y_own(sent)
+    y_more(sent)
     e2own(sent, False)
     for i in range(1, Z):
         e1(i, sent, False)
@@ -534,18 +535,16 @@
     vmem = pl.BlockSpec(memory_space=pltpu.VMEM)
     hbm = pl.BlockSpec(memory_space=pl.ANY)
     dma = pltpu.SemaphoreType.DMA
-    values, token_grad, new_ad, new_m1, new_m2, refreshed = pl.pallas_call(
+    values, token_grad, g, refreshed = pl.pallas_call(
         functools.partial(step_kernel, T, F, scale),
         out_shape=(
             jax.ShapeDtypeStruct((rows, kv), bf16),
             jax.ShapeDtypeStruct((rows, width), bf16),
             jax.ShapeDtypeStruct(flat, f32),
-            jax.ShapeDtypeStruct(flat, f32),
-            jax.ShapeDtypeStruct(flat, f32),
             jax.ShapeDtypeStruct((T * rank, F * sw), bf16),
         ),
         in_specs=[vmem, vmem, vmem, hbm, hbm, hbm, hbm, hbm],
-        out_specs=(vmem, hbm, vmem, vmem, vmem, vmem),
+        out_specs=(vmem, hbm, vmem, vmem),
         scratch_shapes=[
             pltpu.VMEM((F,) + value_weight.shape, bf16),
             pltpu.VMEM(tokens.shape, bf16),
@@ -573,10 +572,15 @@
         pick, mask, adapters.reshape(flat), value_weight, tokens, cotangent,
         first_moment.reshape(flat), second_moment.reshape(flat),
     )
-    shape = adapters.shape
+    g = g.reshape(adapters.shape)
+    new_m1 = beta_first * first_moment + (1.0 - beta_first) * g
+    new_m2 = beta_second * second_moment + (1.0 - beta_second) * g * g
+    new_ad = adapters - learn_rate * (new_m1 / corr_first) / (
+        jnp.sqrt(new_m2 / corr_second) + adam_eps
+    )
     return (
-        values, token_grad, new_ad.reshape(shape), new_m1.reshape(shape),
-        new_m2.reshape(shape), refreshed.reshape(T, rank, F * sw),
+        values, token_grad, new_ad, new_m1, new_m2,
+        refreshed.reshape(T, rank, F * sw),
     )
 
 

time: 198 us -> 172 us (0.87)
  the two profiles are of different devices: /device:TPU:0 before, /device:TPU:29 now
where the time goes in v2:
time: 172 us
  Pallas kernels  152 us (88%)
  local copies, waits for them, and re-layouts  11.7 us (7%)
  other arithmetic  7.86 us (5%)
    pallas_call x1, Pallas kernels, kernel_device(): pl.pallas_call(functools.partial(step_kernel, T, F, scale), out_shape=(ja...  152 us
    unnamed x7, local copies, waits for them, and re-layouts  9.86 us
    sub x1, other arithmetic, kernel_device(): adapters - learn_rate * (new_m1 / corr_first) / (jnp.sqrt(new_m2 / corr_s...  4.64 us

profile of v2, /device:TPU:29, one launch (start us, length us, event | category | flops | bytes accessed | tf_op | source)
XLA Modules:
  0.0 172.2 jit_solution(601918175598765257)
XLA Ops:
  0.6 0.7 dynamic-slice_bitcast_fusion
  1.3 0.8 select_reduce_fusion
  2.2 0.1 broadcast_in_dim.25
  2.2 0.1 mul.47
  2.3 0.8 fusion.1.pick
  3.2 0.9 dynamic-slice_reduce_fusion
  4.1 0.1 broadcast_in_dim.26
  4.1 0.1 eq.55
  4.2 1.5 compare_convert_fusion.mask
  5.7 151.9 %shard_map.136 = (bf16[512,1024]{1,0:T(8,128)(2,1)}, bf16[512,8192]{1,0:T(8,128)(2,1)}, f32[256,1152]{1,0:T(8,128)}, bf16[64,9216]{1,0:T(8,128)(2,1)}) custom-call(bf16[512,256]{1,0:T(8,128)(2,1)} %fusion.1.pick, f32[512,64]{1,0:T(8,128)} %compare_convert_fusion.mask, f32[256,1152]{1,0:T(8,128)} %bitcast.7, bf16[1024,1024]{1,0:T(8,128)(2,1)} %w_hbm.1, ...), custom_call_target="tpu_custom_call" | custom-call | tf_op jit(solution)/shard_map/pallas_call | solution.py:538
  157.7 0.0 copy-start.1
  157.7 4.6 %divide_subtract_fusion = (f32[16,16,1152]{2,1,0:T(8,128)}, f32[16,16,1152]{2,1,0:T(8,128)}, f32[16,16,1152]{2,1,0:T(8,128)}) fusion(f32[16,16,1152]{2,1,0:T(8,128)} %param.12, f32[16,16,1152]{2,1,0:T(8,128)} %bitcast.11, f32[16,16,1152]{2,1,0:T(8,128)} %param.13, f32[16,16,1152]{2,1,0:T(8,128)} %param.14), kind=kLoop, calls=%fused_computation.2 | loop fusion | flops 3538944 | bytes 8257536 | tf_op jit(solution)/shard_map/sub | solution.py:578
  162.3 0.0 copy-done.1
  162.3 1.0 copy.18
  163.3 0.0 copy-start
  163.3 7.9 %copy.19 = bf16[512,8192]{1,0:T(8,128)(2,1)} copy(bf16[512,8192]{1,0:T(8,128)(2,1)} %get-tuple-element.24) | data formatting | bytes 16777216
  171.2 0.0 copy-done
  171.2 1.0 copy.20
  (2 shorter events, 0.0 us)
Async XLA Ops:
  157.7 4.7 %copy-start.1 = (bf16[512,1024]{1,0:T(8,128)(2,1)S(1)}, bf16[512,1024]{1,0:T(8,128)(2,1)}, u32[]{:S(2)}) copy-start(bf16[512,1024]{1,0:T(8,128)(2,1)} %get-tuple-element.23) | copy-start | bytes 3145732
  163.3 7.9 %copy-start = (bf16[64,9216]{1,0:T(8,128)(2,1)S(1)}, bf16[64,9216]{1,0:T(8,128)(2,1)}, u32[]{:S(2)}) copy-start(bf16[64,9216]{1,0:T(8,128)(2,1)} %get-tuple-element.13) | copy-start | bytes 3538948
